TPU v7x, 256 devices: a whole 4x4x8 slice. The times are simulated.
256 devices in a mesh: rep: 8 (over z_lo, y), inner: 32 (over z_hi, x, core).
Axes of the slice: x: 4, y: 4, z: 8 (z_hi: 4, z_lo: 2; z = z_hi * 2 + z_lo), core: 2. Of those that a mesh axis runs over, the one named last changes fastest.
Arguments:
- local_weights: float32 [8, 12, 1600, 1600], P('rep', None, 'inner'), may hold values from -6 to 6
- owner_global: float32 [32, 1600, 1600], P('inner', None, 'rep'), may hold values from -6 to 6
- owner_momentum: float32 [32, 1600, 1600], P('inner', None, 'rep'), may hold values from -6 to 6
- owner_list: int32 [12], replicated, may hold values from 0 to 31, as said below
- local_down: float32 [8, 6400, 1600], P('rep', 'inner'), may hold values from -6 to 6
- global_down: float32 [6400, 1600], P('inner', 'rep'), may hold values from -6 to 6
- down_basis: float32 [6400, 64], P('inner'), may hold values from -0.15625 to 0.15625
- coef_momentum: float32 [64, 1600], P(None, 'rep'), may hold values from -6 to 6
Outputs:
- new_weights: float32 [12, 1600, 1600], P(None, 'inner')
- momentum_out: float32 [32, 1600, 1600], P('inner', None, 'rep')
- new_down: float32 [6400, 1600], P('inner', 'rep')
- coef_new: float32 [64, 1600], P(None, 'rep')
Inputs may be any that keep to these rules, and one draw needn't show every extreme that they name: `owner_list`: the 12 entries are distinct inner indices; both ends of the range are owners.
All inputs are finite; a program needn't handle non-finite values.
Results may differ from a plain program's by a relative error of at most 0.00007.
Values sent between devices are 32-bit elements; how exact they have to be, the bound alone decides.
A program may use at most 128 MiB of HBM per device.

v0:
```python
import jax
import jax.numpy as jnp
from jax import lax
from jax.sharding import PartitionSpec as P

outer_momentum = 0.9
outer_rate = 0.7


def project_rows(basis, values):
    return lax.dot_general(
        basis,
        values,
        (((0,), (0,)), ((), ())),
        precision=lax.Precision.HIGHEST,
        preferred_element_type=jnp.float32,
    )


def on_device(
    local_weights,
    owner_global,
    owner_momentum,
    owner_list,
    local_down,
    global_down,
    down_basis,
    coef_momentum,
):
    groups = lax.axis_size("rep")
    owners = lax.axis_size("inner")
    inner_index = lax.axis_index("inner")
    width = global_down.shape[1]
    col_start = lax.axis_index("rep") * width
    block = local_weights[0]
    matrices = block.shape[0]
    slab = block.shape[1]
    order = jnp.arange(matrices, dtype=jnp.int32)
    match = (owner_list[None, :] == jnp.arange(owners, dtype=jnp.int32)[:, None]).astype(jnp.int32)
    owned = (jnp.sum(match, axis=1) > 0).astype(jnp.float32)
    picked = jnp.sum(match * order[None, :], axis=1)
    down_local = project_rows(down_basis, local_down[0])
    down_global = project_rows(down_basis, global_down)
    summed = lax.psum_scatter(block, "rep", scatter_dimension=2, tiled=True)
    placed = lax.dynamic_update_slice_in_dim(jnp.zeros_like(down_local), down_global, col_start, 1)
    total = lax.psum(placed - down_local / groups, ("rep", "inner"))
    coef_step = lax.dynamic_slice_in_dim(total, col_start, width, 1)
    average = summed / groups
    current = owner_global[0]
    moment = owner_momentum[0]
    outgoing = average[picked] * owned[:, None, None]
    arrived = lax.all_to_all(outgoing, "inner", split_axis=0, concat_axis=0, tiled=True).reshape(
        owners * slab, width
    )
    delta = current - arrived
    moment_new = outer_momentum * moment + delta
    theta = current - outer_rate * (delta + outer_momentum * moment_new)
    is_owner = jnp.sum((owner_list == inner_index).astype(jnp.float32))
    momentum_out = (moment_new * is_owner)[None]
    returned = lax.all_to_all(
        theta.reshape(owners, slab, width), "inner", split_axis=0, concat_axis=0, tiled=True
    )
    updated = returned[owner_list]
    new_weights = lax.all_gather(updated, "rep", axis=2, tiled=True)
    coef_new = outer_momentum * coef_momentum + coef_step
    change = jnp.dot(
        down_basis,
        coef_step + outer_momentum * coef_new,
        precision=lax.Precision.HIGHEST,
        preferred_element_type=jnp.float32,
    )
    new_down = global_down - outer_rate * change
    return (new_weights, momentum_out, new_down, coef_new)


def solution(mesh):
    in_specs = (
        P("rep", None, "inner", None),
        P("inner", None, "rep"),
        P("inner", None, "rep"),
        P(),
        P("rep", "inner", None),
        P("inner", "rep"),
        P("inner", None),
        P(None, "rep"),
    )
    out_specs = (P(None, "inner", None), P("inner", None, "rep"), P("inner", "rep"), P(None, "rep"))
    return jax.shard_map(
        on_device, mesh=mesh, in_specs=in_specs, out_specs=out_specs, check_vma=False
    )
```

profile of v0, /device:TPU:4, one launch (start us, length us, event | category | flops | bytes accessed | tf_op | source)
XLA Modules:
  0.0 588.5 jit_solution(15279377533316422879)
XLA Ops:
  8.0 0.0 copy-start
  8.0 0.0 all-reduce.6.cloned.1.call-start
  8.1 4.6 copy.44
  12.7 0.0 all-reduce.6.cloned.1.call-update
  12.7 0.6 copy-done.7
  13.4 0.6 dynamic-slice
  14.6 0.0 copy-done.6
  14.6 0.1 convert_reduce_fusion
  14.7 117.2 %all-reduce.6.cloned.1.call-done = f32[12,50,1600]{2,1,0:T(8,128)} async-done(((f32[12,50,1600]{2,1,0:T(8,128)}), f32[12,50,1600]{2,1,0:T(8,128)}) %all-reduce.6.cloned.1.call-update) | async-done | bytes 3840016
  132.0 1.5 dynamic-slice_multiply_fusion
  133.4 1.9 gather_fusion
  135.3 2.9 broadcast_multiply_fusion
  138.2 9.2 %all-to-all-start = ((f32[32,50,200]{2,1,0:T(8,128)}), f32[32,50,200]{2,1,0:T(8,128)S(1)}, u32[]{:S(2)}, u32[]{:S(2)}) async-start(f32[32,50,200]{2,1,0:T(8,128)} %broadcast_multiply_fusion), calls=%async_computation | async-start | bytes 3670016 | tf_op jit(solution)/shard_map/all_to_all | solution.py:52
  147.5 3.0 copy.32
  150.5 3.0 copy.33
  153.5 2.6 squeeze.10
  156.1 0.6 fusion.8
  156.7 36.5 %all-to-all-done = f32[32,50,200]{2,1,0:T(8,128)S(1)} async-done(((f32[32,50,200]{2,1,0:T(8,128)}), f32[32,50,200]{2,1,0:T(8,128)S(1)}, u32[]{:S(2)}, u32[]{:S(2)}) %all-to-all-start) | async-done | bytes 1280032 | tf_op jit(solution)/shard_map/all_to_all | solution.py:52
  193.2 1.4 reshape.35
  194.6 5.1 add_multiply_fusion
  199.6 2.6 mul.65
  202.2 3.8 multiply_subtract_fusion
  206.1 5.1 all-to-all-start.1
  211.2 0.0 all-reduce.4.cloned.1.call-start
  211.2 0.0 copy-done.2
  211.2 0.0 copy-done.3
  211.3 0.2 fusion.12
  211.5 0.8 broadcast_in_dim.5
  212.3 1.5 dynamic_update_slice.3
  213.8 0.0 copy-done
  213.8 2.7 fusion
  216.5 0.0 all-reduce.4.cloned.1.call-update
  216.5 0.0 all-gather.3.cloned.1.call-start
  216.6 36.6 %all-to-all-done.1 = f32[32,50,200]{2,1,0:T(8,128)S(1)} async-done(((f32[32,50,200]{2,1,0:T(8,128)}), f32[32,50,200]{2,1,0:T(8,128)S(1)}, u32[]{:S(2)}, u32[]{:S(2)}) %all-to-all-start.1) | async-done | bytes 1280032 | tf_op jit(solution)/shard_map/all_to_all | solution.py:60
  253.2 1.4 gather_fusion.1
  254.6 3.1 copy.34
  257.7 0.0 all-gather.3.cloned.1.call-update
  257.7 0.8 copy.36
  258.5 307.0 %all-reduce.4.cloned.1.call-done = f32[64,1600]{1,0:T(8,128)} async-done(((f32[64,1600]{1,0:T(8,128)}), f32[64,1600]{1,0:T(8,128)}) %all-reduce.4.cloned.1.call-update) | async-done | bytes 409616 | tf_op jit(solution)/shard_map/psum | solution.py:46
  565.5 0.0 copy-done.5
  565.5 1.0 multiply_add_fusion
  566.5 0.0 copy-start.4
  566.5 1.4 fusion.3
  568.0 0.8 copy.39
  568.8 0.0 copy-done.1
  568.8 1.6 copy.38
  570.3 0.0 copy-done.4
  570.3 10.7 %copy.37 = f32[12,50,1600]{2,1,0:T(8,128)} copy(f32[12,50,1600]{1,0,2:T(8,128)} %all-gather.3.cloned.1.call-done) | data formatting | bytes 7680000
  (12 shorter events, 0.0 us)
Async XLA Ops:
  8.0 205.8 %copy-start = (f32[1,200,1600]{2,1,0:T(8,128)S(1)}, f32[1,200,1600]{2,1,0:T(8,128)}, u32[]{:S(2)}) copy-start(f32[1,200,1600]{2,1,0:T(8,128)} %param.12) | copy-start | bytes 3840004
  8.0 124.0 %all-reduce.6.cloned.1.call-start = ((), (), s32[]{:S(2)}) async-start(), calls=%async_computation.4 | async-start | bytes 8945664
  12.7 0.7 copy-start.7
  12.7 1.9 copy-start.6
  138.2 55.0 %all-to-all-start = ((f32[32,50,200]{2,1,0:T(8,128)}), f32[32,50,200]{2,1,0:T(8,128)S(1)}, u32[]{:S(2)}, u32[]{:S(2)}) async-start(f32[32,50,200]{2,1,0:T(8,128)} %broadcast_multiply_fusion), calls=%async_computation | async-start | bytes 3670016 | tf_op jit(solution)/shard_map/all_to_all | solution.py:52
  206.1 5.2 copy-start.2
  206.1 5.2 copy-start.3
  206.1 47.1 %all-to-all-start.1 = ((f32[32,50,200]{2,1,0:T(8,128)}), f32[32,50,200]{2,1,0:T(8,128)S(1)}, u32[]{:S(2)}, u32[]{:S(2)}) async-start(f32[32,50,200]{2,1,0:T(8,128)} %multiply_subtract_fusion), calls=%async_computation.1 | async-start | bytes 3670016 | tf_op jit(solution)/shard_map/all_to_all | solution.py:60
  211.2 354.3 %all-reduce.4.cloned.1.call-start = ((), (), s32[]{:S(2)}) async-start(), calls=%async_computation.2 | async-start | bytes 851968 | tf_op jit(solution)/shard_map/psum | solution.py:46
  216.5 353.8 %all-gather.3.cloned.1.call-start = ((), (), s32[]{:S(2)}) async-start(), calls=%async_computation.3 | async-start | bytes 14745600 | tf_op jit(solution)/shard_map/all_gather | solution.py:64
  254.6 310.9 %copy-start.5 = (f32[64,200]{1,0:T(8,128)S(1)}, f32[64,200]{1,0:T(8,128)}, u32[]{:S(2)}) copy-start(f32[64,200]{1,0:T(8,128)} %param.15) | copy-start | bytes 153604
  257.7 311.0 %copy-start.1 = (f32[1,1600,200]{2,1,0:T(8,128)S(1)}, f32[1,1600,200]{2,1,0:T(8,128)}, u32[]{:S(2)}) copy-start(f32[1,1600,200]{2,1,0:T(8,128)} %get-tuple-element.22) | copy-start | bytes 3840004
  566.5 3.8 copy-start.4
Sparse Core Ops, SparseCore 0:
  12.9 119.0 all-reduce.5
  257.9 139.3 all-gather.2
Sparse Core Ops, SparseCore 1:
  218.1 347.4 all-reduce.3
where the time goes:
time: 589 us; the launch traced here: 588 us
  waiting for transfers between devices  497 us (84%)
  local copies, waits for them, and re-layouts  41 us (7%)
  between operations  16.3 us (3%)
  other arithmetic  15 us (3%)
  starting transfers between devices  14.5 us (2%)
    psum x1, waiting for transfers between devices, on_device(): total = lax.psum(placed - down_local / groups, ('rep', 'inner'))  307 us
    unnamed x4, waiting for transfers between devices  117 us
    all_to_all x1, waiting for transfers between devices, on_device(): lax.all_to_all(theta.reshape(owners, slab, width), 'inner', split_axis=0,...  36.6 us
    all_to_all x1, waiting for transfers between devices, on_device(): lax.all_to_all(outgoing, 'inner', split_axis=0, concat_axis=0, tiled=True)  36.5 us
    unnamed x24, local copies, waits for them, and re-layouts  25.8 us
  transfers between devices with their start and end apart: 5, of which 4 were waited for; matrix products, arithmetic and copies ran while one was open for 4% of the time, Pallas kernels for 0%

commit v1 on v0

--- a/solution.py
+++ b/solution.py
@@ -43,7 +43,7 @@
     down_global = project_rows(down_basis, global_down)
     summed = lax.psum_scatter(block, "rep", scatter_dimension=2, tiled=True)
     placed = lax.dynamic_update_slice_in_dim(jnp.zeros_like(down_local), down_global, col_start, 1)
-    total = lax.psum(placed - down_local / groups, ("rep", "inner"))
+    total = lax.psum(lax.psum(placed - down_local / groups, "inner"), "rep")
     coef_step = lax.dynamic_slice_in_dim(total, col_start, width, 1)
     average = summed / groups
     current = owner_global[0]

time: 589 us -> 701 us (1.19)
  waiting for transfers between devices: 497 us -> 612 us
    all_gather x1, waiting for transfers between devices: 0.01 us -> 130 us  [on_device(): new_weights = lax.all_gather(updated, 'rep', axis=2, tiled=True)]
    psum x1, waiting for transfers between devices: 307 us -> 270 us  [on_device(): total = lax.psum(lax.psum(placed - down_local / groups, 'inner'), 'rep')]
    unnamed x4, waiting for transfers between devices: 117 us -> 130 us
    all_to_all x1, waiting for transfers between devices: 36.6 us -> 45.8 us  [on_device(): lax.all_to_all(theta.reshape(owners, slab, width), 'inner', split_axis=0,...]
    unnamed x24 -> x22, local copies, waits for them, and re-layouts: 25.8 us -> 25 us
  transfers between devices with their start and end apart: 5 -> 5, of which waited for: 4 -> 5; matrix products, arithmetic and copies ran while one was open for 4% -> 3% of each run, Pallas kernels for 0% -> 0%
where the time goes in v1:
time: 701 us; the launch traced here: 700 us
  waiting for transfers between devices  612 us (87%)
  local copies, waits for them, and re-layouts  38.7 us (6%)
  other arithmetic  15.2 us (2%)
  between operations  14.6 us (2%)
  starting transfers between devices  14.3 us (2%)
    psum x1, waiting for transfers between devices, on_device(): total = lax.psum(lax.psum(placed - down_local / groups, 'inner'), 'rep')  270 us
    unnamed x4, waiting for transfers between devices  130 us
    all_gather x1, waiting for transfers between devices, on_device(): new_weights = lax.all_gather(updated, 'rep', axis=2, tiled=True)  130 us
    all_to_all x1, waiting for transfers between devices, on_device(): lax.all_to_all(theta.reshape(owners, slab, width), 'inner', split_axis=0,...  45.8 us
    all_to_all x1, waiting for transfers between devices, on_device(): lax.all_to_all(outgoing, 'inner', split_axis=0, concat_axis=0, tiled=True)  36.6 us
    unnamed x22, local copies, waits for them, and re-layouts  25 us
  transfers between devices with their start and end apart: 5, of which 5 were waited for; matrix products, arithmetic and copies ran while one was open for 3% of the time, Pallas kernels for 0%

profile of v1, /device:TPU:4, one launch (start us, length us, event | category | flops | bytes accessed | tf_op | source)
XLA Modules:
  0.0 699.7 jit_solution(12990792709297339533)
XLA Ops:
  7.2 0.0 copy-start
  7.2 0.0 all-reduce.5.cloned.1.call-start
  7.2 1.3 fusion.12
  8.6 0.7 dynamic_update_slice.3
  9.2 0.0 copy-done
  9.2 2.5 fusion
  11.7 0.0 all-reduce.5.cloned.1.call-update
  11.8 0.0 all-reduce.7.cloned.1.call-start
  11.8 4.5 copy.44
  16.4 269.5 %all-reduce.5.cloned.1.call-done = f32[64,1600]{1,0:T(8,128)} async-done(((f32[64,1600]{1,0:T(8,128)}), f32[64,1600]{1,0:T(8,128)}) %all-reduce.5.cloned.1.call-update) | async-done | bytes 409616 | tf_op jit(solution)/shard_map/psum | solution.py:46
  285.9 0.0 copy-start.6
  285.9 0.0 all-reduce.7.cloned.1.call-update
  285.9 0.6 copy-done.6
  286.6 0.6 dynamic-slice
  287.8 0.0 copy-done.5
  287.8 0.1 convert_reduce_fusion
  287.9 130.2 %all-reduce.7.cloned.1.call-done = (f32[12,50,1600]{2,1,0:T(8,128)}, f32[64,1600]{1,0:T(8,128)}) async-done(((f32[12,50,1600]{2,1,0:T(8,128)}, f32[64,1600]{1,0:T(8,128)}), (f32[12,50,1600]{2,1,0:T(8,128)}, f32[64,1600]{1,0:T(8,128)})) %all-reduce.7.cloned.1.call-update) | async-done | bytes 4249616
  418.2 1.5 dynamic-slice_multiply_fusion
  419.7 1.9 gather_fusion
  421.5 2.9 broadcast_multiply_fusion
  424.5 9.2 %all-to-all-start = ((f32[32,50,200]{2,1,0:T(8,128)}), f32[32,50,200]{2,1,0:T(8,128)S(1)}, u32[]{:S(2)}, u32[]{:S(2)}) async-start(f32[32,50,200]{2,1,0:T(8,128)} %broadcast_multiply_fusion), calls=%async_computation | async-start | bytes 3670016 | tf_op jit(solution)/shard_map/all_to_all | solution.py:52
  433.7 3.0 copy.32
  436.7 3.0 copy.33
  439.7 2.6 squeeze.10
  442.3 0.6 fusion.8
  442.9 36.6 %all-to-all-done = f32[32,50,200]{2,1,0:T(8,128)S(1)} async-done(((f32[32,50,200]{2,1,0:T(8,128)}), f32[32,50,200]{2,1,0:T(8,128)S(1)}, u32[]{:S(2)}, u32[]{:S(2)}) %all-to-all-start) | async-done | bytes 1280032 | tf_op jit(solution)/shard_map/all_to_all | solution.py:52
  479.4 1.4 reshape.35
  480.8 5.1 add_multiply_fusion
  485.9 2.6 mul.65
  488.5 3.8 multiply_subtract_fusion
  492.3 5.0 all-to-all-start.1
  497.3 0.0 all-gather.3.cloned.1.call-start
  497.4 45.8 %all-to-all-done.1 = f32[32,50,200]{2,1,0:T(8,128)S(1)} async-done(((f32[32,50,200]{2,1,0:T(8,128)}), f32[32,50,200]{2,1,0:T(8,128)S(1)}, u32[]{:S(2)}, u32[]{:S(2)}) %all-to-all-start.1) | async-done | bytes 1280032 | tf_op jit(solution)/shard_map/all_to_all | solution.py:60
  543.2 1.4 gather_fusion.1
  544.6 3.1 copy.34
  547.7 0.0 all-gather.3.cloned.1.call-update
  547.7 0.0 copy-done.2
  547.7 0.1 copy.36
  547.9 1.1 multiply_add_fusion
  549.0 0.0 copy-done.3
  549.0 0.0 copy-start.4
  549.0 1.4 fusion.3
  550.4 0.8 copy.39
  551.2 0.0 copy-done.1
  551.2 1.6 copy.38
  552.7 0.0 copy-done.4
  552.7 129.7 %all-gather.3.cloned.1.call-done = f32[12,50,1600]{1,0,2:T(8,128)} async-done(((f32[12,50,200]{1,0,2:T(8,128)}), f32[12,50,1600]{1,0,2:T(8,128)}) %all-gather.3.cloned.1.call-update) | async-done | bytes 3840016 | tf_op jit(solution)/shard_map/all_gather | solution.py:64
  682.4 10.7 %copy.37 = f32[12,50,1600]{2,1,0:T(8,128)} copy(f32[12,50,1600]{1,0,2:T(8,128)} %all-gather.3.cloned.1.call-done) | data formatting | bytes 7680000
  (10 shorter events, 0.1 us)
Async XLA Ops:
  7.2 2.1 copy-start
  7.2 278.7 %all-reduce.5.cloned.1.call-start = ((), (), s32[]{:S(2)}) async-start(), calls=%async_computation.2 | async-start | bytes 851968 | tf_op jit(solution)/shard_map/psum | solution.py:46
  11.8 406.4 %all-reduce.7.cloned.1.call-start = ((), (), s32[]{:S(2)}) async-start(), calls=%async_computation.4 | async-start | bytes 9797632
  285.9 0.7 copy-start.6
  285.9 1.9 copy-start.5
  424.5 55.0 %all-to-all-start = ((f32[32,50,200]{2,1,0:T(8,128)}), f32[32,50,200]{2,1,0:T(8,128)S(1)}, u32[]{:S(2)}, u32[]{:S(2)}) async-start(f32[32,50,200]{2,1,0:T(8,128)} %broadcast_multiply_fusion), calls=%async_computation | async-start | bytes 3670016 | tf_op jit(solution)/shard_map/all_to_all | solution.py:52
  492.3 50.8 %all-to-all-start.1 = ((f32[32,50,200]{2,1,0:T(8,128)}), f32[32,50,200]{2,1,0:T(8,128)S(1)}, u32[]{:S(2)}, u32[]{:S(2)}) async-start(f32[32,50,200]{2,1,0:T(8,128)} %multiply_subtract_fusion), calls=%async_computation.1 | async-start | bytes 3670016 | tf_op jit(solution)/shard_map/all_to_all | solution.py:60
  497.3 185.1 %all-gather.3.cloned.1.call-start = ((), (), s32[]{:S(2)}) async-start(), calls=%async_computation.3 | async-start | bytes 14745600 | tf_op jit(solution)/shard_map/all_gather | solution.py:64
  544.6 3.1 copy-start.2
  544.6 4.4 copy-start.3
  547.7 3.5 copy-start.1
  549.0 3.7 copy-start.4
Sparse Core Ops, SparseCore 0:
  11.9 273.9 all-reduce.4
  289.5 128.6 all-reduce.6
  547.9 134.5 all-gather.2
